TPU v7x, 32 devices: a whole 2x2x4 slice. The times are simulated.
32 devices in a mesh: group: 4 (over z), seq: 8 (over y, x, core).
Axes of the slice: x: 2, y: 2, z: 4, core: 2. Of those that a mesh axis runs over, the one named last changes fastest.
Arguments:
- vis_query: bfloat16 [8, 32, 1280], P('group', 'seq'), parts along dimension 0, may hold values from -200 to 200
- vis_key: bfloat16 [8, 32, 1280], P('group', 'seq'), parts along dimension 0, may hold values from -200 to 200
- vis_value: bfloat16 [8, 32, 1280], P('group', 'seq'), parts along dimension 0, may hold values from -6 to 6
- vis_resid: bfloat16 [8, 32, 1280], P('group', 'seq'), parts along dimension 0, may hold values from -6 to 6
- attn_gate: float32 [1], replicated, may hold values from 0.3 to 1.5
- tile_count: int32 [8], P('group'), parts along dimension 0, may hold values from 1 to 4
- w_kv: bfloat16 [1280, 2048], replicated, may hold values from -0.15625 to 0.15625
- text_query: bfloat16 [4096, 6144], P(('group', 'seq')), parts along dimension 0, may hold values from -200 to 200
- text_image: int32 [4096], P(('group', 'seq')), parts along dimension 0, may hold values from 0 to 1, as said below
Outputs:
- vision_out: bfloat16 [8, 32, 1280], P('group', 'seq'), parts along dimension 0
- cross_out: bfloat16 [4096, 6144], P(('group', 'seq')), parts along dimension 0
There are 4 independent parts, one for each index of `group`. A program takes and returns all parts, laid end to end along the dimension named above; an argument that names none is the same for every part. Nothing has to cross between parts.
Inputs may be any that keep to these rules, and one draw needn't show every extreme that they name: `text_image`: does not fall along the sequence; both values occur.
All inputs are finite; a program needn't handle non-finite values.
Results may differ from a plain program's by a relative error of at most 0.0035.
The roundings to bfloat16 on the way count: a program that leaves them out, or rounds other values in their place, can miss the bound.
Values may be sent and summed in bfloat16 or wider, within the bound.
A program may use at most 64 MiB of HBM per device.

v0:
```python
import math

import jax
import jax.numpy as jnp
from jax import lax
from jax.sharding import PartitionSpec as P

VHEADS = 16
VHEAD = 80
KVH = 8
HD = 128
QGROUP = 6
TILES = 4


def vision_attend(query, keys, values, tile_count, nheads):
    images, rows, width = query.shape
    length = keys.shape[1]
    patch = length // TILES
    tile_of = jnp.arange(length, dtype=jnp.int32) // patch
    key_ok = tile_of[None, :] < tile_count[:, None]
    query = query.reshape(images, rows, nheads, VHEAD)
    keys = keys.reshape(images, length, nheads, VHEAD)
    values = values.reshape(images, length, nheads, VHEAD)
    scores = jnp.einsum(
        "bqhd,bkhd->bhqk", query, keys, preferred_element_type=jnp.float32
    ) / math.sqrt(VHEAD)
    scores = jnp.where(key_ok[:, None, None, :], scores, -1e30)
    peak = jnp.max(scores, axis=-1, keepdims=True)
    expo = jnp.exp(scores - peak)
    probs = (expo / jnp.sum(expo, axis=-1, keepdims=True)).astype(jnp.bfloat16)
    attn = jnp.einsum("bhqk,bkhd->bqhd", probs, values, preferred_element_type=jnp.float32)
    return attn.reshape(images, rows, width)


def on_device(
    vis_query, vis_key, vis_value, vis_resid, attn_gate, tile_count, w_kv, text_query, text_image
):
    images, rows, width = vis_query.shape
    keys, values = (
        lax.all_gather(vis_key, "seq", axis=1, tiled=True),
        lax.all_gather(vis_value, "seq", axis=1, tiled=True),
    )
    attn = vision_attend(vis_query, keys, values, tile_count, VHEADS)
    vision_out = (vis_resid.astype(jnp.float32) + jnp.tanh(attn_gate[0]) * attn).astype(
        jnp.bfloat16
    )
    local_kv = jnp.dot(
        vision_out.reshape(images * rows, width), w_kv, preferred_element_type=jnp.float32
    )
    local_kv = local_kv.astype(jnp.bfloat16).reshape(images, rows, w_kv.shape[1])
    cross_kv = lax.all_gather(local_kv, "seq", axis=1, tiled=True)
    length = cross_kv.shape[1]
    patch = length // TILES
    tile_of = jnp.arange(length, dtype=jnp.int32) // patch
    key_ok = tile_of[None, :] < tile_count[:, None]
    half = KVH * HD
    flat_kv = cross_kv.reshape(images * length, 2 * half)
    cross_key = flat_kv[:, :half].reshape(images * length, KVH, HD)
    cross_value = flat_kv[:, half:].reshape(images * length, KVH, HD)
    image_of_key = jnp.arange(images * length, dtype=jnp.int32) // length
    flat_ok = key_ok.reshape(images * length)
    tokens = text_query.shape[0]
    qrows = text_query.reshape(tokens, KVH, QGROUP, HD)
    score = jnp.einsum(
        "tgqd,kgd->tgqk", qrows, cross_key, preferred_element_type=jnp.float32
    ) / math.sqrt(HD)
    allowed = (image_of_key[None, :] <= text_image[:, None]) & flat_ok[None, :]
    score = jnp.where(allowed[:, None, None, :], score, -1e30)
    top = jnp.max(score, axis=-1, keepdims=True)
    expd = jnp.exp(score - top)
    prob = (expd / jnp.sum(expd, axis=-1, keepdims=True)).astype(jnp.bfloat16)
    out = jnp.einsum("tgqk,kgd->tgqd", prob, cross_value, preferred_element_type=jnp.float32)
    cross_out = out.reshape(tokens, KVH * QGROUP * HD).astype(jnp.bfloat16)
    return (vision_out, cross_out)


def solution(mesh):
    placed = (
        P("group", "seq", None),
        P("group", "seq", None),
        P("group", "seq", None),
        P("group", "seq", None),
        P(),
        P("group"),
        P(),
        P(("group", "seq"), None),
        P(("group", "seq")),
    )
    return jax.shard_map(
        on_device,
        mesh=mesh,
        in_specs=placed,
        out_specs=(P("group", "seq", None), P(("group", "seq"), None)),
        check_vma=False,
    )
```

profile of v0, /device:TPU:0, one launch (start us, length us, event | category | flops | bytes accessed | tf_op | source)
XLA Modules:
  0.0 42.9 jit_solution(13066706277722352874)
XLA Ops:
  0.6 0.0 copy-start.2
  1.3 0.7 %broadcast_compare_fusion = pred[2,32]{1,0:T(4,128)(4,1)S(1)} fusion(s32[32]{0:T(128)S(1)} %and_select_fusion.1, s32[2]{0:T(128)} %param.14), kind=kLoop, calls=%fused_computation.35 | loop fusion | flops 64 | bytes 200 | tf_op jit(solution)/shard_map/lt | solution.py:21
  2.1 0.1 lt.34
  2.2 0.7 %compare_and_fusion = pred[128,64]{0,1:T(8,128)(4,1)S(1)} fusion(s32[128]{0:T(128)} %param.17, s32[64]{0:T(128)S(1)} %and_select_fusion, pred[64]{0:T(512)(128)(4,1)S(1)} %lt.34), kind=kLoop, calls=%fused_computation.25 | loop fusion | flops 16384 | bytes 9024 | tf_op jit(solution)/shard_map/and | solution.py:68
  2.9 0.7 %copy.37 = bf16[2,4,1280]{2,0,1:T(2,128)(2,1)S(1)} copy(bf16[2,4,1280]{2,1,0:T(4,128)(2,1)} %param.10) | data formatting | bytes 40960 | tf_op args[1]
  3.7 0.7 %copy.41 = bf16[2,4,1280]{2,0,1:T(2,128)(2,1)S(1)} copy(bf16[2,4,1280]{2,1,0:T(4,128)(2,1)} %param.11) | data formatting | bytes 40960 | tf_op args[2]
  4.4 0.8 %reshape.139 = bf16[2,4,16,80]{3,2,1,0:T(8,128)(2,1)S(1)} reshape(bf16[2,4,1280]{2,1,0:T(4,128)(2,1)} %param.9) | data formatting | bytes 40960 | tf_op jit(solution)/shard_map/reshape | solution.py:22
  5.2 10.7 %all_gather.10 = bf16[2,32,1280]{2,0,1:T(2,128)(2,1)S(1)} all-gather(bf16[2,4,1280]{2,0,1:T(2,128)(2,1)S(1)} %copy.41), channel_id=1, replica_groups=mesh['group'=4,'seq'=8] {'seq'}, dimensions={1}, use_global_device_ids=true | all-gather | bytes 184320 | tf_op jit(solution)/shard_map/all_gather | solution.py:42
  16.0 0.3 reshape.151
  16.3 9.2 %all_gather.9 = bf16[2,32,1280]{2,0,1:T(2,128)(2,1)S(1)} all-gather(bf16[2,4,1280]{2,0,1:T(2,128)(2,1)S(1)} %copy.37), channel_id=1, replica_groups=mesh['group'=4,'seq'=8] {'seq'}, dimensions={1}, use_global_device_ids=true | all-gather | bytes 184320 | tf_op jit(solution)/shard_map/all_gather | solution.py:41
  25.5 0.3 reshape.150
  25.8 0.3 fusion.7
  26.1 0.2 fusion.16
  26.3 0.5 %fusion.6 = f32[2,4,16,80]{3,1,2,0:T(4,128)S(1)} fusion(bf16[2,32,16,80]{3,2,0,1:T(8,128)(2,1)S(1)} %reshape.151, f32[2,16,4]{2,1,0:T(8,128)S(1)} %fusion.16, f32[]{:T(128)} %bitcast, f32[2,16,4,32]{3,2,1,0:T(4,128)S(1)} %fusion.7), kind=kOutput, calls=%fused_computation.11 | convolution fusion | flops 678047 | bytes 221700 | tf_op jit(solution)/shard_map/bhqk,bkhd->bqhd/dot_general | solution.py:32
  26.8 0.1 mul.15
  27.0 0.0 copy-done.2
  27.0 0.0 copy-start.1
  27.0 3.3 %convolution_convert_fusion = bf16[8,2048]{1,0:T(8,128)(2,1)S(1)} fusion(bf16[8,1280]{1,0:T(8,128)(2,1)S(1)} %reshape.142, bf16[1280,2048]{1,0:T(8,128)(2,1)} %param.15), kind=kOutput, calls=%fused_computation.2 | convolution fusion | flops 41959424 | bytes 5296128 | tf_op jit(solution)/shard_map/dot_general | solution.py:48
  30.3 0.0 copy-done.1
  30.3 0.0 copy-start
  30.4 8.5 %all_gather.11 = bf16[2,32,2048]{2,0,1:T(2,128)(2,1)S(1)} all-gather(bf16[2,4,2048]{2,0,1:T(2,128)(2,1)S(1)} %copy.45), channel_id=1, replica_groups=mesh['group'=4,'seq'=8] {'seq'}, dimensions={1}, use_global_device_ids=true | all-gather | bytes 294912 | tf_op jit(solution)/shard_map/all_gather | solution.py:52
  38.8 0.1 copy.46
  39.0 0.0 copy-done
  39.0 0.9 %copy.47 = bf16[128,6144]{0,1:T(8,128)(2,1)S(1)} copy(bf16[128,6144]{1,0:T(8,128)(2,1)S(1)} %copy-done) | data formatting | bytes 3145728 | tf_op args[7]
  39.9 0.4 bitcast_select_fusion
  40.3 0.3 fusion.17
  40.6 0.6 %convolution_convert_fusion.1 = bf16[8,128,128,6]{2,1,3,0:T(8,128)(2,1)S(1)} fusion(f32[128,8,6]{0,2,1:T(8,128)S(1)} %fusion.17, bf16[64,8,128,1]{2,1,0,3:T(8,128)(2,1)S(1)} %bitcast.37, f32[128,8,6,64]{0,3,2,1:T(8,128)S(1)} %bitcast_select_fusion), kind=kOutput, calls=%fused_computation.4 | convolution fusion | flops 102635584 | bytes 3301376 | tf_op jit(solution)/shard_map/tgqk,kgd->tgqd/dot_general | solution.py:73
  41.3 1.6 %copy.51 = bf16[128,6144]{1,0:T(8,128)(2,1)} copy(bf16[128,6144]{0,1:T(8,128)(2,1)S(1)} %bitcast.34) | data formatting | bytes 3145728
  (10 shorter events, 0.2 us)
Async XLA Ops:
  0.6 26.3 %copy-start.2 = (bf16[2,4,1280]{2,1,0:T(4,128)(2,1)S(1)}, bf16[2,4,1280]{2,1,0:T(4,128)(2,1)}, u32[]{:S(2)}) copy-start(bf16[2,4,1280]{2,1,0:T(4,128)(2,1)} %param.12) | copy-start | bytes 61444
  27.0 3.3 %copy-start.1 = (bf16[2,4,1280]{2,1,0:T(4,128)(2,1)}, bf16[2,4,1280]{2,1,0:T(4,128)(2,1)S(1)}, u32[]{:S(2)}) copy-start(bf16[2,4,1280]{2,1,0:T(4,128)(2,1)S(1)} %add_convert_fusion) | copy-start | bytes 61444
  30.3 8.7 %copy-start = (bf16[128,6144]{1,0:T(8,128)(2,1)S(1)}, bf16[128,6144]{1,0:T(8,128)(2,1)}, u32[]{:S(2)}) copy-start(bf16[128,6144]{1,0:T(8,128)(2,1)} %param.16) | copy-start | bytes 4718596
where the time goes:
time: 43.3 us; the launch traced here: 42.9 us
  blocking collectives  28.4 us (66%)
  local copies, waits for them, and re-layouts  5.82 us (13%)
  matrix products  5.08 us (12%)
  other arithmetic  2.02 us (5%)
  between operations  1.5 us (3%)
    all_gather x1, blocking collectives, on_device(): lax.all_gather(vis_value, 'seq', axis=1, tiled=True)  10.7 us
    all_gather x1, blocking collectives, on_device(): lax.all_gather(vis_key, 'seq', axis=1, tiled=True)  9.23 us
    all_gather x1, blocking collectives, on_device(): cross_kv = lax.all_gather(local_kv, 'seq', axis=1, tiled=True)  8.46 us
    unnamed x13, local copies, waits for them, and re-layouts  4.04 us
    dot_general x1, matrix products, on_device(): jnp.dot(vision_out.reshape(images * rows, width), w_kv, preferred_element...  3.27 us

commit v1 on v0

--- a/solution.py
+++ b/solution.py
@@ -1,8 +1,11 @@
+import functools
 import math
 
 import jax
 import jax.numpy as jnp
 from jax import lax
+from jax.experimental import pallas as pl
+from jax.experimental.pallas import tpu as pltpu
 from jax.sharding import PartitionSpec as P
 
 VHEADS = 16
@@ -11,6 +14,8 @@
 HD = 128
 QGROUP = 6
 TILES = 4
+LANES = 128
+NEG = -1e30
 
 
 def vision_attend(query, keys, values, tile_count, nheads):
@@ -25,7 +30,7 @@
     scores = jnp.einsum(
         "bqhd,bkhd->bhqk", query, keys, preferred_element_type=jnp.float32
     ) / math.sqrt(VHEAD)
-    scores = jnp.where(key_ok[:, None, None, :], scores, -1e30)
+    scores = jnp.where(key_ok[:, None, None, :], scores, NEG)
     peak = jnp.max(scores, axis=-1, keepdims=True)
     expo = jnp.exp(scores - peak)
     probs = (expo / jnp.sum(expo, axis=-1, keepdims=True)).astype(jnp.bfloat16)
@@ -33,7 +38,7 @@
     return attn.reshape(images, rows, width)
 
 
-def on_device(
+def general_form(
     vis_query, vis_key, vis_value, vis_resid, attn_gate, tile_count, w_kv, text_query, text_image
 ):
     images, rows, width = vis_query.shape
@@ -66,13 +71,275 @@
         "tgqd,kgd->tgqk", qrows, cross_key, preferred_element_type=jnp.float32
     ) / math.sqrt(HD)
     allowed = (image_of_key[None, :] <= text_image[:, None]) & flat_ok[None, :]
-    score = jnp.where(allowed[:, None, None, :], score, -1e30)
+    score = jnp.where(allowed[:, None, None, :], score, NEG)
     top = jnp.max(score, axis=-1, keepdims=True)
     expd = jnp.exp(score - top)
     prob = (expd / jnp.sum(expd, axis=-1, keepdims=True)).astype(jnp.bfloat16)
     out = jnp.einsum("tgqk,kgd->tgqd", prob, cross_value, preferred_element_type=jnp.float32)
     cross_out = out.reshape(tokens, KVH * QGROUP * HD).astype(jnp.bfloat16)
     return (vision_out, cross_out)
+
+
+def key_facts(index, images, rows, length, counts):
+    image = (index // rows) % images
+    place = (index // (images * rows)) * rows + index % rows
+    tile = place // (length // TILES)
+    count = jnp.zeros_like(index)
+    for b in range(images):
+        count = jnp.where(image == b, counts[b], count)
+    return image, tile < count
+
+
+def vision_kernel(
+    n, images, rows, width,
+    gate_ref, count_ref, q_in, k_in, v_in, r_in, w_in,
+    out_ref, kv_ref,
+    slots, stage, w_vmem, vis_all, load_sem, w_sem, send_sem, recv_sem,
+):
+    me = lax.axis_index("seq")
+    chips = n // 2
+    half = chips // 2
+    chip, core = me // 2, me % 2
+    partner = chip * 2 + (1 - core)
+    block = images * rows
+    total = n * block
+
+    w_copy = pltpu.make_async_copy(w_in, w_vmem, w_sem)
+    loads = [
+        pltpu.make_async_copy(ref, slots.at[me, a], load_sem.at[a])
+        for a, ref in enumerate((q_in, k_in, v_in, r_in))
+    ]
+    for load in loads:
+        load.start()
+
+    peers = []
+    for ky in reversed(range(half)):
+        for kx in reversed(range(2)):
+            if ky or kx:
+                there = ((chip // 2 + ky) % half) * 2 + (chip % 2 + kx) % 2
+                peers.append((there * 2 + core, there * 2 + (1 - core)))
+
+    def signal(dev, sem):
+        pl.semaphore_signal(
+            sem, inc=1, device_id={"seq": dev}, device_id_type=pl.DeviceIdType.MESH
+        )
+
+    barrier = pltpu.get_barrier_semaphore()
+    for dev, _ in peers:
+        signal(dev, barrier)
+    signal(partner, barrier)
+    w_copy.start()
+    pl.semaphore_wait(barrier, len(peers) + 1)
+    for load in loads:
+        load.wait()
+
+    def send(slot, dev, number):
+        return pltpu.make_async_remote_copy(
+            src_ref=slots.at[slot],
+            dst_ref=slots.at[slot],
+            send_sem=send_sem.at[number],
+            recv_sem=recv_sem.at[slot],
+            device_id={"seq": dev},
+            device_id_type=pl.DeviceIdType.MESH,
+        )
+
+    sent = [send(me, dev, i) for i, (dev, _) in enumerate(peers)]
+    sent.append(send(me, partner, len(peers)))
+    for copy in sent:
+        copy.start()
+
+    def unpack(slot):
+        at = pl.multiple_of(slot * block, block)
+        for a in range(4):
+            pieces = [slots[slot, a, b].astype(jnp.float32) for b in range(images)]
+            stage[a, pl.ds(at, block), :] = jnp.concatenate(pieces, axis=0)
+
+    def arrived(slot):
+        send(slot, partner, 0).wait_recv()
+
+    unpack(me)
+    arrived(partner)
+    unpack(partner)
+    for i, (dev, _) in reversed(list(enumerate(peers))):
+        arrived(dev)
+        relay = send(dev, partner, len(peers) + 1 + i)
+        relay.start()
+        sent.append(relay)
+        unpack(dev)
+    for dev, other in reversed(peers):
+        arrived(other)
+        unpack(other)
+
+    length = n * rows
+    counts = [count_ref[b] for b in range(images)]
+    k_index = lax.broadcasted_iota(jnp.int32, (total, total), 1)
+    q_index = lax.broadcasted_iota(jnp.int32, (total, total), 0)
+    k_image, k_ok = key_facts(k_index, images, rows, length, counts)
+    q_image = (q_index // rows) % images
+    ok = (k_image == q_image) & k_ok
+    heads = width // VHEAD
+    query = stage[0].astype(jnp.bfloat16)
+    key = stage[1].astype(jnp.bfloat16)
+    value = stage[2].astype(jnp.bfloat16)
+    parts = [None] * (width // LANES)
+    for h in range(heads):
+        first, last = h * VHEAD, (h + 1) * VHEAD
+        t0, t1 = first // LANES, -(-last // LANES)
+        lo, hi = t0 * LANES, t1 * LANES
+        lane = lax.broadcasted_iota(jnp.int32, (total, hi - lo), 1) + lo
+        mine = (lane >= first) & (lane < last)
+        zero = jnp.zeros((), jnp.bfloat16)
+        k_h = jnp.where(mine, key[:, lo:hi], zero)
+        v_h = jnp.where(mine, value[:, lo:hi], zero)
+        score = lax.dot_general(
+            query[:, lo:hi], k_h, (((1,), (1,)), ((), ())), preferred_element_type=jnp.float32
+        ) / math.sqrt(VHEAD)
+        score = jnp.where(ok, score, NEG)
+        expo = jnp.exp(score - jnp.max(score, axis=-1, keepdims=True))
+        prob = (expo / jnp.sum(expo, axis=-1, keepdims=True)).astype(jnp.bfloat16)
+        attn = jnp.dot(prob, v_h, preferred_element_type=jnp.float32)
+        for t in range(t0, t1):
+            piece = attn[:, (t - t0) * LANES : (t - t0 + 1) * LANES]
+            parts[t] = piece if parts[t] is None else parts[t] + piece
+    gate = jnp.tanh(jnp.full((1, LANES), gate_ref[0], jnp.float32))
+    for t, part in enumerate(parts):
+        cols = slice(t * LANES, (t + 1) * LANES)
+        vis_all[:, cols] = stage[3, :, cols] + gate * part
+    mine = vis_all[pl.ds(pl.multiple_of(me * block, block), block), :]
+    for b in range(images):
+        out_ref[b] = mine[b * rows : (b + 1) * rows].astype(jnp.bfloat16)
+    vis = vis_all[...].astype(jnp.bfloat16)
+    w_copy.wait()
+    step = 2 * LANES
+    for j in range(w_vmem.shape[1] // step):
+        cols = slice(j * step, (j + 1) * step)
+        kv_ref[:, cols] = jnp.dot(
+            vis, w_vmem[:, cols], preferred_element_type=jnp.float32
+        ).astype(jnp.bfloat16)
+    for copy in sent:
+        copy.wait_send()
+
+
+def vision_part(n, q, k, v, r, gate, count, w_kv):
+    images, rows, width = q.shape
+    total = n * images * rows
+    anyspace = pl.BlockSpec(memory_space=pl.ANY)
+    smem = pl.BlockSpec(memory_space=pltpu.SMEM)
+    vmem = pl.BlockSpec(memory_space=pltpu.VMEM)
+    return pl.pallas_call(
+        functools.partial(vision_kernel, n, images, rows, width),
+        out_shape=(
+            jax.ShapeDtypeStruct(q.shape, jnp.bfloat16),
+            jax.ShapeDtypeStruct((total, w_kv.shape[1]), jnp.bfloat16),
+        ),
+        in_specs=[smem, smem] + [anyspace] * 5,
+        out_specs=(vmem, vmem),
+        scratch_shapes=[
+            pltpu.VMEM((n, 4, images, rows, width), jnp.bfloat16),
+            pltpu.VMEM((4, total, width), jnp.float32),
+            pltpu.VMEM(w_kv.shape, jnp.bfloat16),
+            pltpu.VMEM((total, width), jnp.float32),
+            pltpu.SemaphoreType.DMA((4,)),
+            pltpu.SemaphoreType.DMA,
+            pltpu.SemaphoreType.DMA((n,)),
+            pltpu.SemaphoreType.DMA((n,)),
+        ],
+        compiler_params=pltpu.CompilerParams(collective_id=0, has_side_effects=True),
+        name="vision",
+    )(gate, count, q, k, v, r, w_kv)
+
+
+def text_kernel(
+    images, rows, length, groups,
+    count_ref, seen_ref, vis_ref, q_ref, k_ref, v_ref, vis_out, o_ref, allow_ref,
+):
+    tokens = q_ref.shape[0]
+    keys = images * length
+
+    @pl.when(pl.program_id(0) == 0)
+    def _():
+        vis_out[...] = vis_ref[...]
+        counts = [count_ref[b] for b in range(images)]
+        index = lax.broadcasted_iota(jnp.int32, (tokens, LANES), 1) % keys
+        token = lax.broadcasted_iota(jnp.int32, (tokens, LANES), 0)
+        image, ok = key_facts(index, images, rows, length, counts)
+        seen = seen_ref[...]
+        border = jnp.zeros_like(token)
+        for b in range(1, images):
+            below = jnp.sum((seen < b).astype(jnp.float32), axis=-1, keepdims=True)
+            border = jnp.where(image == b, below.astype(jnp.int32), border)
+        allow_ref[...] = (ok & (token >= border)).astype(jnp.float32)
+
+    allowed = allow_ref[...] > 0.5
+    left = lax.broadcasted_iota(jnp.int32, (tokens, LANES), 1) < keys
+    for g in range(groups):
+        k_g = k_ref[:, g * HD : (g + 1) * HD]
+        v_g = v_ref[:, g * HD : (g + 1) * HD]
+        zero = jnp.zeros_like(k_g)
+        k_two = jnp.concatenate(
+            [jnp.concatenate([k_g, zero], axis=1), jnp.concatenate([zero, k_g], axis=1)], axis=0
+        )
+        v_two = jnp.concatenate(
+            [jnp.concatenate([v_g, zero], axis=1), jnp.concatenate([zero, v_g], axis=1)], axis=0
+        )
+        for j in range(QGROUP // 2):
+            cols = slice((g * QGROUP + 2 * j) * HD, (g * QGROUP + 2 * j + 2) * HD)
+            score = lax.dot_general(
+                q_ref[:, cols], k_two, (((1,), (1,)), ((), ())),
+                preferred_element_type=jnp.float32,
+            ) / math.sqrt(HD)
+            score = jnp.where(allowed, score, NEG)
+            low = jnp.finfo(jnp.float32).min
+            top_l = jnp.max(jnp.where(left, score, low), axis=-1, keepdims=True)
+            top_r = jnp.max(jnp.where(left, low, score), axis=-1, keepdims=True)
+            expd = jnp.exp(score - jnp.where(left, top_l, top_r))
+            sum_l = jnp.sum(jnp.where(left, expd, 0.0), axis=-1, keepdims=True)
+            sum_r = jnp.sum(jnp.where(left, 0.0, expd), axis=-1, keepdims=True)
+            prob = (expd / jnp.where(left, sum_l, sum_r)).astype(jnp.bfloat16)
+            o_ref[:, cols] = jnp.dot(
+                prob, v_two, preferred_element_type=jnp.float32
+            ).astype(jnp.bfloat16)
+
+
+def text_part(n, rows, count, seen, vis, query, kv):
+    images = vis.shape[0]
+    length = n * rows
+    tokens = query.shape[0]
+    groups = 2
+    steps = KVH // groups
+    smem = pl.BlockSpec(memory_space=pltpu.SMEM)
+    vmem = pl.BlockSpec(memory_space=pltpu.VMEM)
+    span = groups * QGROUP * HD
+    return pl.pallas_call(
+        functools.partial(text_kernel, images, rows, length, groups),
+        grid=(steps,),
+        out_shape=(
+            jax.ShapeDtypeStruct(vis.shape, jnp.bfloat16),
+            jax.ShapeDtypeStruct(query.shape, jnp.bfloat16),
+        ),
+        in_specs=[
+            smem,
+            vmem,
+            vmem,
+            pl.BlockSpec((tokens, span), lambda i: (0, i)),
+            pl.BlockSpec((images * length, groups * HD), lambda i: (0, i)),
+            pl.BlockSpec((images * length, groups * HD), lambda i: (0, i + steps)),
+        ],
+        out_specs=(vmem, pl.BlockSpec((tokens, span), lambda i: (0, i))),
+        scratch_shapes=[pltpu.VMEM((tokens, LANES), jnp.float32)],
+        name="text",
+    )(count, seen.reshape(1, tokens), vis, query, kv, kv)
+
+
+def on_device(n, *args):
+    vis_query, vis_key, vis_value, vis_resid, attn_gate, tile_count, w_kv, text_query, text_image = args
+    images, rows, width = vis_query.shape
+    if n % 4 or 2 * images * rows * n != LANES or (images * rows) % 8:
+        return general_form(*args)
+    vis, kv = vision_part(
+        n, vis_query, vis_key, vis_value, vis_resid, attn_gate, tile_count, w_kv
+    )
+    return text_part(n, rows, tile_count, text_image, vis, text_query, kv)
 
 
 def solution(mesh):
@@ -88,7 +355,7 @@
         P(("group", "seq")),
     )
     return jax.shard_map(
-        on_device,
+        functools.partial(on_device, mesh.shape["seq"]),
         mesh=mesh,
         in_specs=placed,
         out_specs=(P("group", "seq", None), P(("group", "seq"), None)),

time: 43.3 us -> 22.4 us (0.52)
  the two profiles are of different devices: /device:TPU:0 before, /device:TPU:1 now
where the time goes in v1:
time: 22.4 us; the launch traced here: 22.2 us
  Pallas kernels  20.9 us (93%)
  between operations  1.29 us (6%)
    pallas_call x1, Pallas kernels, vision_part(): pl.pallas_call(functools.partial(vision_kernel, n, images, rows, width),...  14.7 us
    pallas_call x1, Pallas kernels, text_part(): pl.pallas_call(functools.partial(text_kernel, images, rows, length, group...  6.2 us

profile of v1, /device:TPU:1, one launch (start us, length us, event | category | flops | bytes accessed | tf_op | source)
XLA Modules:
  0.0 22.2 jit_solution(11700899701416770129)
XLA Ops:
  1.3 14.7 %vision.1 = (bf16[2,4,1280]{2,1,0:T(4,128)(2,1)}, bf16[64,2048]{1,0:T(8,128)(2,1)}) custom-call(f32[1]{0:T(128)S(6)} %copy.11.gate_ref, s32[2]{0:T(128)} %count_ref.3, bf16[2,4,1280]{2,1,0:T(4,128)(2,1)} %q_in.1, bf16[2,4,1280]{2,1,0:T(4,128)(2,1)} %k_in.1, bf16[2,4,1280]{2,1,0:T(4,128)(2,1)} %v_in.1, bf16[2,4,1280]{2,1,0:T(4,128)(2,1)} %r_in.1, ...), custom_call_target="tpu_custom_call" | custom-call | tf_op jit(solution)/shard_map/vision/pallas_call | solution.py:229
  16.0 6.2 %text.1 = (bf16[2,4,1280]{2,1,0:T(4,128)(2,1)}, bf16[128,6144]{1,0:T(8,128)(2,1)}) custom-call(s32[2]{0:T(128)} %count_ref.3, s32[1,128]{1,0:T(1,128)} %bitcast.1, bf16[2,4,1280]{2,1,0:T(4,128)(2,1)} %get-tuple-element.4.vis_ref, bf16[128,6144]{1,0:T(8,128)(2,1)} %q_ref.1, bf16[64,2048]{1,0:T(8,128)(2,1)} %get-tuple-element.5.k_ref.v_ref, ...), custom_call_target="tpu_custom_call" | custom-call | tf_op jit(solution)/shard_map/text/pallas_call | solution.py:313

commit v2 on v0

--- a/solution.py
+++ b/solution.py
@@ -1,8 +1,11 @@
+import functools
 import math
 
 import jax
 import jax.numpy as jnp
 from jax import lax
+from jax.experimental import pallas as pl
+from jax.experimental.pallas import tpu as pltpu
 from jax.sharding import PartitionSpec as P
 
 VHEADS = 16
@@ -11,6 +14,8 @@
 HD = 128
 QGROUP = 6
 TILES = 4
+LANES = 128
+NEG = -1e30
 
 
 def vision_attend(query, keys, values, tile_count, nheads):
@@ -25,7 +30,7 @@
     scores = jnp.einsum(
         "bqhd,bkhd->bhqk", query, keys, preferred_element_type=jnp.float32
     ) / math.sqrt(VHEAD)
-    scores = jnp.where(key_ok[:, None, None, :], scores, -1e30)
+    scores = jnp.where(key_ok[:, None, None, :], scores, NEG)
     peak = jnp.max(scores, axis=-1, keepdims=True)
     expo = jnp.exp(scores - peak)
     probs = (expo / jnp.sum(expo, axis=-1, keepdims=True)).astype(jnp.bfloat16)
@@ -33,7 +38,7 @@
     return attn.reshape(images, rows, width)
 
 
-def on_device(
+def general_form(
     vis_query, vis_key, vis_value, vis_resid, attn_gate, tile_count, w_kv, text_query, text_image
 ):
     images, rows, width = vis_query.shape
@@ -66,13 +71,317 @@
         "tgqd,kgd->tgqk", qrows, cross_key, preferred_element_type=jnp.float32
     ) / math.sqrt(HD)
     allowed = (image_of_key[None, :] <= text_image[:, None]) & flat_ok[None, :]
-    score = jnp.where(allowed[:, None, None, :], score, -1e30)
+    score = jnp.where(allowed[:, None, None, :], score, NEG)
     top = jnp.max(score, axis=-1, keepdims=True)
     expd = jnp.exp(score - top)
     prob = (expd / jnp.sum(expd, axis=-1, keepdims=True)).astype(jnp.bfloat16)
     out = jnp.einsum("tgqk,kgd->tgqd", prob, cross_value, preferred_element_type=jnp.float32)
     cross_out = out.reshape(tokens, KVH * QGROUP * HD).astype(jnp.bfloat16)
     return (vision_out, cross_out)
+
+
+GRANT = 16 * 1024 * 1024
+MESH = pl.DeviceIdType.MESH
+
+
+def spare_rows(images, rows):
+    return -(-images * rows // 16) * 16
+
+
+def vision_kernel(
+    n, images, rows, width, tokens,
+    gate_in, count_in, seen_in, q_in, k_in, v_in, r_in, w_in,
+    pack_ref,
+    slots, stage, w_vmem, vis_all, seen_ref, gate_ref, count_ref,
+    load_sem, w_sem, small_sem, send_sem, recv_sem,
+):
+    me = lax.axis_index("seq")
+    chips = n // 2
+    half = chips // 2
+    chip, core = me // 2, me % 2
+    partner = chip * 2 + (1 - core)
+    length = n * rows
+    keys = images * length
+    pair = 2 * rows
+
+    loads = [
+        pltpu.make_async_copy(ref.at[b], slots.at[me, b, a], load_sem.at[b, a])
+        for b in range(images)
+        for a, ref in enumerate((q_in, k_in, v_in, r_in))
+    ]
+    for load in loads:
+        load.start()
+
+    peers = []
+    for ky in range(half):
+        for kx in range(2):
+            if ky or kx:
+                there = ((chip // 2 + ky) % half) * 2 + (chip % 2 + kx) % 2
+                peers.append((there, there * 2 + core, there * 2 + (1 - core)))
+
+    barrier = pltpu.get_barrier_semaphore()
+    for dev in [dev for _, dev, _ in peers] + [partner]:
+        pl.semaphore_signal(barrier, inc=1, device_id={"seq": dev}, device_id_type=MESH)
+    small = [
+        pltpu.make_async_copy(gate_in, gate_ref, small_sem.at[0]),
+        pltpu.make_async_copy(count_in, count_ref, small_sem.at[1]),
+        pltpu.make_async_copy(seen_in, seen_ref, small_sem.at[2]),
+    ]
+    for copy in small:
+        copy.start()
+    w_copy = pltpu.make_async_copy(w_in, w_vmem, w_sem)
+    w_copy.start()
+    pl.semaphore_wait(barrier, len(peers) + 1)
+    for load in loads:
+        load.wait()
+
+    def send(slot, b, dev, number):
+        return pltpu.make_async_remote_copy(
+            src_ref=slots.at[slot, b],
+            dst_ref=slots.at[slot, b],
+            send_sem=send_sem.at[b, number],
+            recv_sem=recv_sem.at[b, slot],
+            device_id={"seq": dev},
+            device_id_type=MESH,
+        )
+
+    sent = []
+    for b in range(images):
+        for number, (_, dev, _) in reversed(list(enumerate(peers))):
+            sent.append(send(me, b, dev, number))
+        sent.append(send(me, b, partner, len(peers)))
+    for copy in sent:
+        copy.start()
+
+    for copy in small:
+        copy.wait()
+    place = lax.broadcasted_iota(jnp.int32, (length, tokens), 0)
+    kv_width = w_vmem.shape[1]
+    for b in range(images):
+        ok = (place // (length // TILES) < count_ref[b]) & (seen_ref[...] >= b)
+        pack_ref[b * length : (b + 1) * length, kv_width : kv_width + tokens] = jnp.where(
+            ok, 0.0, NEG
+        ).astype(jnp.bfloat16)
+    gate = jnp.tanh(jnp.full((1, LANES), gate_ref[0], jnp.float32))
+
+    def arrived(slot, b):
+        send(slot, b, partner, 0).wait_recv()
+
+    def forward(b):
+        for i, (_, dev, _) in enumerate(peers):
+            arrived(dev, b)
+            relay = send(dev, b, partner, len(peers) + 1 + i)
+            relay.start()
+            sent.append(relay)
+
+    def unpack(there, b):
+        at = pl.multiple_of(there * pair, pair)
+        for a in range(4):
+            two = [slots[there * 2 + c, b, a].astype(jnp.float32) for c in range(2)]
+            stage[b, a, pl.ds(at, pair), :] = jnp.concatenate(two, axis=0)
+
+    def gather(b):
+        arrived(partner, b)
+        unpack(chip, b)
+        for there, _, other in peers:
+            arrived(other, b)
+            unpack(there, b)
+
+    heads = width // VHEAD
+    side = LANES // length
+    key_row = lax.broadcasted_iota(jnp.int32, (length, LANES), 0)
+    scale = math.log2(math.e) / math.sqrt(VHEAD)
+
+    def attend(b):
+        query = stage[b, 0].astype(jnp.bfloat16)
+        key = stage[b, 1].astype(jnp.bfloat16)
+        value = stage[b, 2].astype(jnp.bfloat16)
+        bias = jnp.where(key_row // (length // TILES) < count_ref[b], 0.0, NEG)
+        parts = [None] * (width // LANES)
+        for h in range(0, heads, side):
+            t0, t1 = h * VHEAD // LANES, -(-(h + side) * VHEAD // LANES)
+            lo, hi = t0 * LANES, t1 * LANES
+            lane = lax.broadcasted_iota(jnp.int32, (length, hi - lo), 1) + lo
+            own = [
+                (lane >= i * VHEAD) & (lane < (i + 1) * VHEAD) for i in range(h, h + side)
+            ]
+            window = query[:, lo:hi]
+            spread = jnp.concatenate(
+                [jnp.where(mask, window, jnp.zeros_like(window)) for mask in own], axis=0
+            )
+            score = lax.dot_general(
+                key[:, lo:hi], spread, (((1,), (1,)), ((), ())),
+                preferred_element_type=jnp.float32,
+            )
+            score = score + bias
+            expo = jnp.exp2((score - jnp.max(score, axis=0, keepdims=True)) * scale)
+            prob = expo * (1.0 / jnp.sum(expo, axis=0, keepdims=True))
+            attn = lax.dot_general(
+                prob.astype(jnp.bfloat16), value[:, lo:hi], (((0,), (0,)), ((), ())),
+                preferred_element_type=jnp.float32,
+            )
+            total = jnp.zeros((length, hi - lo), jnp.float32)
+            for i, mask in enumerate(own):
+                total = jnp.where(mask, attn[i * length : (i + 1) * length], total)
+            for t in range(t0, t1):
+                piece = total[:, (t - t0) * LANES : (t - t0 + 1) * LANES]
+                parts[t] = piece if parts[t] is None else parts[t] + piece
+        for t, part in enumerate(parts):
+            cols = slice(t * LANES, (t + 1) * LANES)
+            vis_all[b, :, cols] = stage[b, 3, :, cols] + gate * part
+
+    def project(b):
+        vis = vis_all[b].astype(jnp.bfloat16)
+        step = 2 * LANES
+        for j in range(w_vmem.shape[1] // step):
+            cols = slice(j * step, (j + 1) * step)
+            pack_ref[b * length : (b + 1) * length, cols] = jnp.dot(
+                vis, w_vmem[:, cols], preferred_element_type=jnp.float32
+            ).astype(jnp.bfloat16)
+
+    forward(0)
+    gather(0)
+    attend(0)
+    w_copy.wait()
+    for b in range(1, images):
+        forward(b)
+        project(b - 1)
+        gather(b)
+        attend(b)
+    project(images - 1)
+    mine = []
+    for b in range(images):
+        near = vis_all[b, pl.ds(pl.multiple_of(chip * pair, pair), pair), :]
+        mine.append(jnp.where(core == 0, near[:rows], near[rows:]))
+    mine.extend([jnp.zeros_like(mine[0])] * (spare_rows(images, rows) // rows - images))
+    pack_ref[keys:, :width] = jnp.concatenate(mine, axis=0).astype(jnp.bfloat16)
+    for copy in sent:
+        copy.wait_send()
+
+
+def vision_part(n, q, k, v, r, gate, count, seen, w_kv):
+    images, rows, width = q.shape
+    length = n * rows
+    keys = images * length
+    tokens = seen.shape[0]
+    anyspace = pl.BlockSpec(memory_space=pltpu.HBM)
+    vmem = pl.BlockSpec(memory_space=pltpu.VMEM)
+    return pl.pallas_call(
+        functools.partial(vision_kernel, n, images, rows, width, tokens),
+        out_shape=jax.ShapeDtypeStruct(
+            (keys + spare_rows(images, rows), w_kv.shape[1] + tokens), jnp.bfloat16
+        ),
+        in_specs=[anyspace] * 8,
+        out_specs=vmem,
+        scratch_shapes=[
+            pltpu.VMEM((n, images, 4, rows, width), jnp.bfloat16),
+            pltpu.VMEM((images, 4, length, width), jnp.float32),
+            pltpu.VMEM(w_kv.shape, jnp.bfloat16),
+            pltpu.VMEM((images, length, width), jnp.float32),
+            pltpu.VMEM((1, tokens), jnp.int32),
+            pltpu.SMEM((1,), jnp.float32),
+            pltpu.SMEM((images,), jnp.int32),
+            pltpu.SemaphoreType.DMA((images, 4)),
+            pltpu.SemaphoreType.DMA,
+            pltpu.SemaphoreType.DMA((3,)),
+            pltpu.SemaphoreType.DMA((images, n)),
+            pltpu.SemaphoreType.DMA((images, n)),
+        ],
+        compiler_params=pltpu.CompilerParams(
+            collective_id=0, has_side_effects=True
+        ),
+        name="vision",
+    )(gate, count, seen.reshape(1, tokens), q, k, v, r, w_kv)
+
+
+def text_kernel(pack_ref, q_ref, vis_out, out_hbm, o_ref, bias_ref, out_sem):
+    images, rows, width = vis_out.shape
+    keys, tokens = bias_ref.shape[0] // 2, bias_ref.shape[1]
+    for b in range(images):
+        vis_out[b] = pack_ref[keys + b * rows : keys + (b + 1) * rows, :width]
+    for twin in range(2):
+        bias_ref[twin * keys : (twin + 1) * keys, :] = pack_ref[
+            :keys, 2 * KVH * HD : 2 * KVH * HD + tokens
+        ].astype(jnp.float32)
+    scale = math.log2(math.e) / math.sqrt(HD)
+    span = QGROUP * HD
+    copies = []
+    for g in range(KVH):
+        k_g = pack_ref[:keys, g * HD : (g + 1) * HD]
+        v_g = pack_ref[:keys, (KVH + g) * HD : (KVH + g + 1) * HD]
+        zero = jnp.zeros_like(k_g)
+        k_two = jnp.concatenate(
+            [jnp.concatenate([k_g, zero], axis=1), jnp.concatenate([zero, k_g], axis=1)], axis=0
+        )
+        v_two = jnp.concatenate(
+            [jnp.concatenate([v_g, zero], axis=1), jnp.concatenate([zero, v_g], axis=1)], axis=0
+        )
+        for j in range(QGROUP // 2):
+            cols = slice(g * span + 2 * j * HD, g * span + (2 * j + 2) * HD)
+            score = lax.dot_general(
+                k_two, q_ref[:, cols], (((1,), (1,)), ((), ())),
+                preferred_element_type=jnp.float32,
+            )
+            score = score + bias_ref[...]
+            probs = []
+            for part in (score[:keys], score[keys:]):
+                expd = jnp.exp2((part - jnp.max(part, axis=0, keepdims=True)) * scale)
+                probs.append(expd * (1.0 / jnp.sum(expd, axis=0, keepdims=True)))
+            prob = jnp.concatenate(probs, axis=0).astype(jnp.bfloat16)
+            o_ref[:, cols] = lax.dot_general(
+                prob, v_two, (((0,), (0,)), ((), ())), preferred_element_type=jnp.float32
+            ).astype(jnp.bfloat16)
+        cols = pl.ds(g * span, span)
+        copies.append(
+            pltpu.make_async_copy(o_ref.at[:, cols], out_hbm.at[:, cols], out_sem.at[g])
+        )
+        copies[-1].start()
+    for copy in copies:
+        copy.wait()
+
+
+def text_part(shape, keys, pack, query):
+    vmem = pl.BlockSpec(memory_space=pltpu.VMEM)
+    return pl.pallas_call(
+        text_kernel,
+        out_shape=(
+            jax.ShapeDtypeStruct(shape, jnp.bfloat16),
+            jax.ShapeDtypeStruct(query.shape, jnp.bfloat16),
+        ),
+        in_specs=[vmem] * 2,
+        out_specs=(vmem, pl.BlockSpec(memory_space=pl.ANY)),
+        scratch_shapes=[
+            pltpu.VMEM(query.shape, jnp.bfloat16),
+            pltpu.VMEM((2 * keys, query.shape[0]), jnp.float32),
+            pltpu.SemaphoreType.DMA((KVH,)),
+        ],
+        compiler_params=pltpu.CompilerParams(vmem_limit_bytes=GRANT),
+        name="text",
+    )(pack, query)
+
+
+def fits(n, images, rows, width):
+    length = n * rows
+    return (
+        n % 4 == 0
+        and 2 * images * length == LANES
+        and LANES % length == 0
+        and (width // VHEAD) % (LANES // length) == 0
+        and (2 * rows) % 8 == 0
+        and length % 16 == 0
+        and spare_rows(images, rows) % rows == 0
+    )
+
+
+def on_device(n, *args):
+    vis_query, vis_key, vis_value, vis_resid, attn_gate, tile_count, w_kv, text_query, text_image = args
+    images, rows, width = vis_query.shape
+    if not fits(n, images, rows, width):
+        return general_form(*args)
+    pack = vision_part(
+        n, vis_query, vis_key, vis_value, vis_resid, attn_gate, tile_count, text_image, w_kv
+    )
+    return text_part(vis_query.shape, images * rows * n, pack, text_query)
 
 
 def solution(mesh):
@@ -88,7 +397,7 @@
         P(("group", "seq")),
     )
     return jax.shard_map(
-        on_device,
+        functools.partial(on_device, mesh.shape["seq"]),
         mesh=mesh,
         in_specs=placed,
         out_specs=(P("group", "seq", None), P(("group", "seq"), None)),

time: 43.3 us -> 19.3 us (0.45)
  blocking collectives: 28.4 us -> 0 us
  Pallas kernels: 0 us -> 16.9 us
  matrix products: 5.08 us -> 0 us
  local copies, waits for them, and re-layouts: 5.82 us -> 0.98 us
  other arithmetic: 2.02 us -> 0 us
    all_gather x3 -> x0, blocking collectives: 28.4 us -> none  [the longest x1 10.7 us: on_device(): lax.all_gather(vis_value, 'seq', axis=1, tiled=True)]
    pallas_call x0 -> x2, Pallas kernels: none -> 16.9 us  [the longest x1 14.1 us: vision_part(): pl.pallas_call(functools.partial(vision_kernel, n, images, rows, width, t...]
    dot_general x5 -> x0, matrix products: 5.08 us -> none  [the longest x1 3.27 us: on_device(): jnp.dot(vision_out.reshape(images * rows, width), w_kv, preferred_element...]
    unnamed x13 -> x4, local copies, waits for them, and re-layouts: 4.04 us -> 0.98 us
    reshape x6 -> x0, local copies, waits for them, and re-layouts: 1.49 us -> none  [the longest x1 0.83 us: vision_attend(): query = query.reshape(images, rows, nheads, VHEAD)]
    and x1 -> x0, other arithmetic: 0.73 us -> none  [on_device(): allowed = (image_of_key[None, :] <= text_image[:, None]) & flat_ok[None, :]]
    lt x1 -> x0, other arithmetic: 0.73 us -> none  [vision_attend(): key_ok = tile_of[None, :] < tile_count[:, None]]
    sub x2 -> x0, other arithmetic: 0.54 us -> none  [the longest x1 0.33 us: on_device(): expd = jnp.exp(score - top)]
where the time goes in v2:
time: 19.3 us; the launch traced here: 19.2 us
  Pallas kernels  16.9 us (88%)
  between operations  1.31 us (7%)
  local copies, waits for them, and re-layouts  0.98 us (5%)
    pallas_call x1, Pallas kernels, vision_part(): pl.pallas_call(functools.partial(vision_kernel, n, images, rows, width, t...  14.1 us
    pallas_call x1, Pallas kernels, text_part(): pl.pallas_call(text_kernel, out_shape=(jax.ShapeDtypeStruct(shape, jnp.bf...  2.79 us
    unnamed x4, local copies, waits for them, and re-layouts  0.98 us

profile of v2, /device:TPU:0, one launch (start us, length us, event | category | flops | bytes accessed | tf_op | source)
XLA Modules:
  0.0 19.2 jit_solution(6074773015223281676)
XLA Ops:
  1.3 0.0 copy-start
  1.3 14.1 %vision.1.pack_ref = bf16[80,2176]{1,0:T(8,128)(2,1)} custom-call(f32[1]{0:T(128)S(6)} %copy.11.gate_in, s32[2]{0:T(128)} %count_in.1, s32[1,128]{1,0:T(1,128)} %bitcast.1, bf16[2,4,1280]{2,1,0:T(4,128)(2,1)} %q_in.1, bf16[2,4,1280]{2,1,0:T(4,128)(2,1)} %k_in.1, bf16[2,4,1280]{2,1,0:T(4,128)(2,1)} %v_in.1, bf16[2,4,1280]{2,1,0:T(4,128)(2,1)} %r_in.1, ...), custom_call_target="tpu_custom_call" | custom-call | tf_op jit(solution)/shard_map/vision/pallas_call | solution.py:269
  15.4 0.0 copy-done
  15.4 0.0 copy-start.1
  15.4 1.0 %copy-done.1 = bf16[80,2176]{1,0:T(8,128)(2,1)S(1)} copy-done((bf16[80,2176]{1,0:T(8,128)(2,1)S(1)}, bf16[80,2176]{1,0:T(8,128)(2,1)}, u32[]{:S(2)}) %copy-start.1) | copy-done | bytes 348184
  16.4 2.8 %text.1 = (bf16[2,4,1280]{2,1,0:T(4,128)(2,1)}, bf16[128,6144]{1,0:T(8,128)(2,1)}) custom-call(bf16[80,2176]{1,0:T(8,128)(2,1)S(1)} %copy-done.1, bf16[128,6144]{1,0:T(8,128)(2,1)S(1)} %copy-done), custom_call_target="tpu_custom_call" | custom-call | tf_op jit(solution)/shard_map/text/pallas_call | solution.py:345
Async XLA Ops:
  1.3 14.1 %copy-start = (bf16[128,6144]{1,0:T(8,128)(2,1)S(1)}, bf16[128,6144]{1,0:T(8,128)(2,1)}, u32[]{:S(2)}) copy-start(bf16[128,6144]{1,0:T(8,128)(2,1)} %q_ref.1) | copy-start | bytes 4718596
  15.4 1.0 %copy-start.1 = (bf16[80,2176]{1,0:T(8,128)(2,1)S(1)}, bf16[80,2176]{1,0:T(8,128)(2,1)}, u32[]{:S(2)}) copy-start(bf16[80,2176]{1,0:T(8,128)(2,1)} %vision.1.pack_ref) | copy-start | bytes 1044484

commit v3 on v2

--- a/solution.py
+++ b/solution.py
@@ -91,9 +91,9 @@
 def vision_kernel(
     n, images, rows, width, tokens,
     gate_in, count_in, seen_in, q_in, k_in, v_in, r_in, w_in,
-    pack_ref,
-    slots, stage, w_vmem, vis_all, seen_ref, gate_ref, count_ref,
-    load_sem, w_sem, small_sem, send_sem, recv_sem,
+    pack_hbm,
+    pack_ref, slots, stage, w_vmem, vis_all, seen_ref, gate_ref, count_ref,
+    load_sem, w_sem, small_sem, send_sem, recv_sem, out_sem,
 ):
     me = lax.axis_index("seq")
     chips = n // 2
@@ -162,6 +162,16 @@
         pack_ref[b * length : (b + 1) * length, kv_width : kv_width + tokens] = jnp.where(
             ok, 0.0, NEG
         ).astype(jnp.bfloat16)
+    out = []
+
+    def write(at_rows, at_cols):
+        copy = pltpu.make_async_copy(
+            pack_ref.at[at_rows, at_cols], pack_hbm.at[at_rows, at_cols], out_sem.at[len(out)]
+        )
+        copy.start()
+        out.append(copy)
+
+    write(pl.ds(0, keys), pl.ds(kv_width, tokens))
     gate = jnp.tanh(jnp.full((1, LANES), gate_ref[0], jnp.float32))
 
     def arrived(slot, b):
@@ -238,6 +248,8 @@
             pack_ref[b * length : (b + 1) * length, cols] = jnp.dot(
                 vis, w_vmem[:, cols], preferred_element_type=jnp.float32
             ).astype(jnp.bfloat16)
+            if b == images - 1:
+                write(pl.ds(0, keys), pl.ds(j * step, step))
 
     forward(0)
     gather(0)
@@ -248,13 +260,16 @@
         project(b - 1)
         gather(b)
         attend(b)
-    project(images - 1)
     mine = []
     for b in range(images):
         near = vis_all[b, pl.ds(pl.multiple_of(chip * pair, pair), pair), :]
         mine.append(jnp.where(core == 0, near[:rows], near[rows:]))
     mine.extend([jnp.zeros_like(mine[0])] * (spare_rows(images, rows) // rows - images))
     pack_ref[keys:, :width] = jnp.concatenate(mine, axis=0).astype(jnp.bfloat16)
+    write(pl.ds(keys, spare_rows(images, rows)), pl.ds(0, width))
+    project(images - 1)
+    for copy in out:
+        copy.wait()
     for copy in sent:
         copy.wait_send()
 
@@ -265,15 +280,15 @@
     keys = images * length
     tokens = seen.shape[0]
     anyspace = pl.BlockSpec(memory_space=pltpu.HBM)
-    vmem = pl.BlockSpec(memory_space=pltpu.VMEM)
     return pl.pallas_call(
         functools.partial(vision_kernel, n, images, rows, width, tokens),
         out_shape=jax.ShapeDtypeStruct(
             (keys + spare_rows(images, rows), w_kv.shape[1] + tokens), jnp.bfloat16
         ),
         in_specs=[anyspace] * 8,
-        out_specs=vmem,
+        out_specs=anyspace,
         scratch_shapes=[
+            pltpu.VMEM((keys + spare_rows(images, rows), w_kv.shape[1] + tokens), jnp.bfloat16),
             pltpu.VMEM((n, images, 4, rows, width), jnp.bfloat16),
             pltpu.VMEM((images, 4, length, width), jnp.float32),
             pltpu.VMEM(w_kv.shape, jnp.bfloat16),
@@ -286,6 +301,7 @@
             pltpu.SemaphoreType.DMA((3,)),
             pltpu.SemaphoreType.DMA((images, n)),
             pltpu.SemaphoreType.DMA((images, n)),
+            pltpu.SemaphoreType.DMA((2 + w_kv.shape[1] // (2 * LANES),)),
         ],
         compiler_params=pltpu.CompilerParams(
             collective_id=0, has_side_effects=True

time: 19.3 us -> 19.3 us (level)
  no operation moved by 1% of the time
where the time goes in v3:
time: 19.3 us; the launch traced here: 19.2 us
  Pallas kernels  16.9 us (88%)
  between operations  1.31 us (7%)
  local copies, waits for them, and re-layouts  0.98 us (5%)
    pallas_call x1, Pallas kernels, vision_part(): pl.pallas_call(functools.partial(vision_kernel, n, images, rows, width, t...  14.1 us
    pallas_call x1, Pallas kernels, text_part(): pl.pallas_call(text_kernel, out_shape=(jax.ShapeDtypeStruct(shape, jnp.bf...  2.79 us
    unnamed x4, local copies, waits for them, and re-layouts  0.98 us

profile of v3, /device:TPU:0, one launch (start us, length us, event | category | flops | bytes accessed | tf_op | source)
XLA Modules:
  0.0 19.2 jit_solution(16034491663998067702)
XLA Ops:
  1.3 0.0 copy-start
  1.3 14.1 %vision.1.pack_ref = bf16[80,2176]{1,0:T(8,128)(2,1)} custom-call(f32[1]{0:T(128)S(6)} %copy.11.gate_in, s32[2]{0:T(128)} %count_in.1, s32[1,128]{1,0:T(1,128)} %bitcast.1, bf16[2,4,1280]{2,1,0:T(4,128)(2,1)} %q_in.1, bf16[2,4,1280]{2,1,0:T(4,128)(2,1)} %k_in.1, bf16[2,4,1280]{2,1,0:T(4,128)(2,1)} %v_in.1, bf16[2,4,1280]{2,1,0:T(4,128)(2,1)} %r_in.1, ...), custom_call_target="tpu_custom_call" | custom-call | tf_op jit(solution)/shard_map/vision/pallas_call | solution.py:283
  15.4 0.0 copy-done
  15.4 0.0 copy-start.1
  15.4 1.0 %copy-done.1 = bf16[80,2176]{1,0:T(8,128)(2,1)S(1)} copy-done((bf16[80,2176]{1,0:T(8,128)(2,1)S(1)}, bf16[80,2176]{1,0:T(8,128)(2,1)}, u32[]{:S(2)}) %copy-start.1) | copy-done | bytes 348184
  16.4 2.8 %text.1 = (bf16[2,4,1280]{2,1,0:T(4,128)(2,1)}, bf16[128,6144]{1,0:T(8,128)(2,1)}) custom-call(bf16[80,2176]{1,0:T(8,128)(2,1)S(1)} %copy-done.1, bf16[128,6144]{1,0:T(8,128)(2,1)S(1)} %copy-done), custom_call_target="tpu_custom_call" | custom-call | tf_op jit(solution)/shard_map/text/pallas_call | solution.py:361
Async XLA Ops:
  1.3 14.1 %copy-start = (bf16[128,6144]{1,0:T(8,128)(2,1)S(1)}, bf16[128,6144]{1,0:T(8,128)(2,1)}, u32[]{:S(2)}) copy-start(bf16[128,6144]{1,0:T(8,128)(2,1)} %q_ref.1) | copy-start | bytes 4718596
  15.4 1.0 %copy-start.1 = (bf16[80,2176]{1,0:T(8,128)(2,1)S(1)}, bf16[80,2176]{1,0:T(8,128)(2,1)}, u32[]{:S(2)}) copy-start(bf16[80,2176]{1,0:T(8,128)(2,1)} %vision.1.pack_ref) | copy-start | bytes 1044484

commit v4 on v2

--- a/solution.py
+++ b/solution.py
@@ -109,9 +109,6 @@
         for b in range(images)
         for a, ref in enumerate((q_in, k_in, v_in, r_in))
     ]
-    for load in loads:
-        load.start()
-
     peers = []
     for ky in range(half):
         for kx in range(2):
@@ -122,6 +119,8 @@
     barrier = pltpu.get_barrier_semaphore()
     for dev in [dev for _, dev, _ in peers] + [partner]:
         pl.semaphore_signal(barrier, inc=1, device_id={"seq": dev}, device_id_type=MESH)
+    for load in loads:
+        load.start()
     small = [
         pltpu.make_async_copy(gate_in, gate_ref, small_sem.at[0]),
         pltpu.make_async_copy(count_in, count_ref, small_sem.at[1]),

time: 19.3 us -> 19.3 us (level)
  no operation moved by 1% of the time
where the time goes in v4:
time: 19.3 us; the launch traced here: 19.1 us
  Pallas kernels  16.9 us (88%)
  between operations  1.31 us (7%)
  local copies, waits for them, and re-layouts  0.98 us (5%)
    pallas_call x1, Pallas kernels, vision_part(): pl.pallas_call(functools.partial(vision_kernel, n, images, rows, width, t...  14.1 us
    pallas_call x1, Pallas kernels, text_part(): pl.pallas_call(text_kernel, out_shape=(jax.ShapeDtypeStruct(shape, jnp.bf...  2.79 us
    unnamed x4, local copies, waits for them, and re-layouts  0.98 us

profile of v4, /device:TPU:0, one launch (start us, length us, event | category | flops | bytes accessed | tf_op | source)
XLA Modules:
  0.0 19.1 jit_solution(2033016674978517590)
XLA Ops:
  1.3 0.0 copy-start
  1.3 14.1 %vision.1.pack_ref = bf16[80,2176]{1,0:T(8,128)(2,1)} custom-call(f32[1]{0:T(128)S(6)} %copy.11.gate_in, s32[2]{0:T(128)} %count_in.1, s32[1,128]{1,0:T(1,128)} %bitcast.1, bf16[2,4,1280]{2,1,0:T(4,128)(2,1)} %q_in.1, bf16[2,4,1280]{2,1,0:T(4,128)(2,1)} %k_in.1, bf16[2,4,1280]{2,1,0:T(4,128)(2,1)} %v_in.1, bf16[2,4,1280]{2,1,0:T(4,128)(2,1)} %r_in.1, ...), custom_call_target="tpu_custom_call" | custom-call | tf_op jit(solution)/shard_map/vision/pallas_call | solution.py:268
  15.4 0.0 copy-done
  15.4 0.0 copy-start.1
  15.4 1.0 %copy-done.1 = bf16[80,2176]{1,0:T(8,128)(2,1)S(1)} copy-done((bf16[80,2176]{1,0:T(8,128)(2,1)S(1)}, bf16[80,2176]{1,0:T(8,128)(2,1)}, u32[]{:S(2)}) %copy-start.1) | copy-done | bytes 348184
  16.4 2.8 %text.1 = (bf16[2,4,1280]{2,1,0:T(4,128)(2,1)}, bf16[128,6144]{1,0:T(8,128)(2,1)}) custom-call(bf16[80,2176]{1,0:T(8,128)(2,1)S(1)} %copy-done.1, bf16[128,6144]{1,0:T(8,128)(2,1)S(1)} %copy-done), custom_call_target="tpu_custom_call" | custom-call | tf_op jit(solution)/shard_map/text/pallas_call | solution.py:344
Async XLA Ops:
  1.3 14.1 %copy-start = (bf16[128,6144]{1,0:T(8,128)(2,1)S(1)}, bf16[128,6144]{1,0:T(8,128)(2,1)}, u32[]{:S(2)}) copy-start(bf16[128,6144]{1,0:T(8,128)(2,1)} %q_ref.1) | copy-start | bytes 4718596
  15.4 1.0 %copy-start.1 = (bf16[80,2176]{1,0:T(8,128)(2,1)S(1)}, bf16[80,2176]{1,0:T(8,128)(2,1)}, u32[]{:S(2)}) copy-start(bf16[80,2176]{1,0:T(8,128)(2,1)} %vision.1.pack_ref) | copy-start | bytes 1044484
